TPU v7x, 32 devices: a whole 2x2x4 slice. The times are simulated.
32 devices in a mesh: rows: 8 (over z, x), cols: 4 (over y, core).
Axes of the slice: x: 2, y: 2, z: 4, core: 2. Of those that a mesh axis runs over, the one named last changes fastest.
Arguments:
- panel_t: float32 [16, 2048], P(None, ('rows', 'cols')), may hold values from -6 to 6
- kinship: float32 [2048, 2048], P('rows', 'cols'), may hold values from -0.125 to 0.125
Outputs:
- kin_panel_t: float32 [16, 2048], P(None, ('rows', 'cols'))
- score: float32 [16, 16], replicated
All inputs are finite; a program needn't handle non-finite values.
Results may differ from a plain program's by a relative error of at most 0.00008.
Values sent between devices are 32-bit elements; how exact they have to be, the bound alone decides.
A program may use at most 64 MiB of HBM per device.

v0:
```python
import jax
import jax.numpy as jnp
from jax import lax
from jax.sharding import PartitionSpec as P


def contract(left, right):
    return lax.dot_general(
        left,
        right,
        (((1,), (1,)), ((), ())),
        precision=lax.Precision.HIGHEST,
        preferred_element_type=jnp.float32,
    )


def shards(panel_t, kinship):
    slab_rows, block_cols = kinship.shape
    row_index = lax.axis_index("rows")
    col_index = lax.axis_index("cols")
    gathered = lax.all_gather(panel_t, ("rows", "cols"), axis=1, tiled=True)
    slab_panel = lax.dynamic_slice_in_dim(gathered, row_index * slab_rows, slab_rows, 1)
    block_panel = lax.dynamic_slice_in_dim(gathered, col_index * block_cols, block_cols, 1)
    partial_value = contract(block_panel, kinship)
    scale = jnp.sqrt(jnp.float32(gathered.shape[1]))
    early_sum = lax.psum(contract(slab_panel, partial_value), ("rows", "cols"))
    kin_panel_t = lax.psum_scatter(partial_value, "cols", scatter_dimension=1, tiled=True)
    return (kin_panel_t, early_sum / scale)


def solution(mesh):
    placed = (P(None, ("rows", "cols")), P("rows", "cols"))
    return jax.shard_map(
        shards,
        mesh=mesh,
        in_specs=placed,
        out_specs=(P(None, ("rows", "cols")), P()),
        check_vma=False,
    )
```

profile of v0, /device:TPU:10, one launch (start us, length us, event | category | flops | bytes accessed | tf_op | source)
XLA Modules:
  0.0 99.6 jit_solution(12220211806638438616)
XLA Ops:
  7.2 0.0 copy-start
  7.2 0.0 reduce-scatter.4.cloned.1.call-start
  7.2 32.8 %all-gather = f32[32,64,16]{1,2,0:T(8,128)S(1)} all-gather(f32[1,64,16]{1,2,0:T(8,128)} %bitcast.11), channel_id=1, replica_groups=mesh['rows'=8,'cols'=4] {'rows','cols'}, dimensions={0}, use_global_device_ids=true | all-gather | bytes 135168 | tf_op jit(solution)/shard_map/all_gather | solution.py:21
  40.1 0.1 copy.5
  40.2 0.1 reshape.5
  40.3 0.0 copy-done
  40.3 0.5 fusion
  40.8 0.8 copy.6
  41.6 0.0 reduce-scatter.4.cloned.1.call-update
  41.6 0.1 fusion.2
  41.7 49.0 %psum.7 = f32[16,16]{1,0:T(8,128)S(1)} all-reduce(f32[16,16]{1,0:T(8,128)S(1)} %fusion.2), channel_id=1, replica_groups=mesh['rows'=8,'cols'=4] {'rows','cols'}, use_global_device_ids=true, to_apply=%region_1.0 | all-reduce | flops 256 | bytes 2048 | tf_op jit(solution)/shard_map/psum | solution.py:26
  90.7 0.6 broadcast_multiply_fusion
  91.3 0.0 reduce-scatter.4.cloned.1.call-done
  91.3 1.4 %copy.7 = f32[16,64]{1,0:T(8,128)} copy(f32[16,64]{0,1:T(8,128)} %bitcast.10) | data formatting | bytes 8192
Async XLA Ops:
  7.2 33.1 %copy-start = (f32[256,512]{1,0:T(8,128)S(1)}, f32[256,512]{1,0:T(8,128)}, u32[]{:S(2)}) copy-start(f32[256,512]{1,0:T(8,128)} %param.3) | copy-start | bytes 1572868
  7.2 84.1 %reduce-scatter.4.cloned.1.call-start = ((), (), s32[]{:S(2)}) async-start(), calls=%async_computation.1 | async-start | bytes 163840
Sparse Core Ops, SparseCore 0:
  41.7 25.6 reduce-scatter.3
where the time goes:
time: 99.9 us; the launch traced here: 99.6 us
  blocking collectives  81.8 us (82%)
  between operations  14.1 us (14%)
  local copies, waits for them, and re-layouts  2.39 us (2%)
    psum x1, blocking collectives, shards(): early_sum = lax.psum(contract(slab_panel, partial_value), ('rows', 'cols'))  49 us
    all_gather x1, blocking collectives, shards(): gathered = lax.all_gather(panel_t, ('rows', 'cols'), axis=1, tiled=True)  32.8 us
    unnamed x5, local copies, waits for them, and re-layouts  2.31 us
  transfers between devices with their start and end apart: 1, of which 0 were waited for; matrix products, arithmetic and copies ran while one was open for 1% of the time, Pallas kernels for 0%

commit v1 on v0

--- a/solution.py
+++ b/solution.py
@@ -23,7 +23,8 @@
     block_panel = lax.dynamic_slice_in_dim(gathered, col_index * block_cols, block_cols, 1)
     partial_value = contract(block_panel, kinship)
     scale = jnp.sqrt(jnp.float32(gathered.shape[1]))
-    early_sum = lax.psum(contract(slab_panel, partial_value), ("rows", "cols"))
+    one_axis = lax.psum(contract(slab_panel, partial_value), "cols")
+    early_sum = lax.psum(one_axis, "rows")
     kin_panel_t = lax.psum_scatter(partial_value, "cols", scatter_dimension=1, tiled=True)
     return (kin_panel_t, early_sum / scale)
 

time: 99.9 us -> 85.8 us (0.86)
  the two profiles are of different devices: /device:TPU:10 before, /device:TPU:0 now
where the time goes in v1:
time: 85.8 us; the launch traced here: 85.6 us
  blocking collectives  67.8 us (79%)
  between operations  14.1 us (16%)
  local copies, waits for them, and re-layouts  2.39 us (3%)
    all_gather x1, blocking collectives, shards(): gathered = lax.all_gather(panel_t, ('rows', 'cols'), axis=1, tiled=True)  44.3 us
    psum x1, blocking collectives, shards(): early_sum = lax.psum(one_axis, 'rows')  17.4 us
    psum x1, blocking collectives, shards(): one_axis = lax.psum(contract(slab_panel, partial_value), 'cols')  6.11 us
    unnamed x5, local copies, waits for them, and re-layouts  2.31 us
  transfers between devices with their start and end apart: 1, of which 0 were waited for; matrix products, arithmetic and copies ran while one was open for 1% of the time, Pallas kernels for 0%

profile of v1, /device:TPU:0, one launch (start us, length us, event | category | flops | bytes accessed | tf_op | source)
XLA Modules:
  0.0 85.6 jit_solution(16316751144760683234)
XLA Ops:
  7.2 0.0 copy-start
  7.2 0.0 reduce-scatter.4.cloned.1.call-start
  7.2 44.3 %all-gather = f32[32,64,16]{1,2,0:T(8,128)S(1)} all-gather(f32[1,64,16]{1,2,0:T(8,128)} %bitcast.11), channel_id=1, replica_groups=mesh['rows'=8,'cols'=4] {'rows','cols'}, dimensions={0}, use_global_device_ids=true | all-gather | bytes 135168 | tf_op jit(solution)/shard_map/all_gather | solution.py:21
  51.6 0.1 copy.5
  51.7 0.1 reshape.5
  51.8 0.0 copy-done
  51.8 0.5 fusion
  52.3 0.8 copy.6
  53.1 0.0 reduce-scatter.4.cloned.1.call-update
  53.1 0.1 fusion.2
  53.2 6.1 %psum.14 = f32[16,16]{1,0:T(8,128)S(1)} all-reduce(f32[16,16]{1,0:T(8,128)S(1)} %fusion.2), channel_id=1, replica_groups=mesh['rows'=8,'cols'=4] {'cols'}, use_global_device_ids=true, to_apply=%region_1.0 | all-reduce | flops 256 | bytes 2048 | tf_op jit(solution)/shard_map/psum | solution.py:26
  59.3 17.4 %psum.15 = f32[16,16]{1,0:T(8,128)S(1)} all-reduce(f32[16,16]{1,0:T(8,128)S(1)} %psum.14), channel_id=1, replica_groups=mesh['rows'=8,'cols'=4] {'rows'}, use_global_device_ids=true, to_apply=%region_2.0 | all-reduce | flops 256 | bytes 2048 | tf_op jit(solution)/shard_map/psum | solution.py:27
  76.7 0.6 broadcast_multiply_fusion
  77.3 0.0 reduce-scatter.4.cloned.1.call-done
  77.3 1.4 %copy.7 = f32[16,64]{1,0:T(8,128)} copy(f32[16,64]{0,1:T(8,128)} %bitcast.10) | data formatting | bytes 8192
Async XLA Ops:
  7.2 44.6 %copy-start = (f32[256,512]{1,0:T(8,128)S(1)}, f32[256,512]{1,0:T(8,128)}, u32[]{:S(2)}) copy-start(f32[256,512]{1,0:T(8,128)} %param.3) | copy-start | bytes 1572868
  7.2 70.1 %reduce-scatter.4.cloned.1.call-start = ((), (), s32[]{:S(2)}) async-start(), calls=%async_computation.1 | async-start | bytes 163840
Sparse Core Ops, SparseCore 0:
  53.2 15.7 reduce-scatter.3
